TPU v7x, 32 devices: a whole 2x2x4 slice. The times are simulated.
32 devices in a mesh: dom: 8 (over z, y), rep: 4 (over x, core).
Axes of the slice: x: 2, y: 2, z: 4, core: 2. Of those that a mesh axis runs over, the one named last changes fastest.
Arguments:
- features: bfloat16 [16384, 768], P(('dom', 'rep')), may hold values from -13 to 13
- sketch_matrix: bfloat16 [768, 256], replicated, may hold values from -0.21875 to 0.21875
- tiles: bfloat16 [8, 20, 256, 256], P('dom'), may hold values from 0 to 2, as said below
- tile_dst: int32 [8, 20], P('dom'), may hold values from -1 to 7, as said below
- tile_src: int32 [8, 20], P('dom'), may hold values from 0 to 11, as said below
- halo_index: int32 [8, 1024], P('dom'), may hold values from 0 to 2047
- send_order: int32 [8, 2048], P('dom'), may hold values from 0 to 2047, each once within a row
- arrival_place: int32 [8, 2048], P('dom'), may hold values from 0 to 2047, each once within a row
Outputs:
- signals: bfloat16 [3, 256, 16384], P(None, 'rep', 'dom')
Inputs may be any that keep to these rules, and one draw needn't show every extreme that they name: `tiles`: entries are zero or positive; in slot t < 8 of every partition the tile's diagonal is positive. `tile_dst`: in every partition slot t < 8 holds t, the live slots come first and the others hold -1; some partition uses every slot and some only the first 12. `tile_src`: slot t < 12 holds t in every partition; empty slots hold 0. `halo_index`: A row may be listed for several peers and more than once. `send_order`: each row is a permutation. `arrival_place`: each row is a permutation.
All inputs are finite; a program needn't handle non-finite values.
Results may differ from a plain program's by a relative error of at most 0.0034.
Values may be sent and summed in bfloat16 or wider, within the bound.
No kernel may reach another device: no remote copies, remote signals or barrier semaphores. Data moves between devices by JAX's collectives and lax.ppermute only.
A program may use at most 64 MiB of HBM per device.

v0:
```python
import jax
import jax.numpy as jnp
from jax import lax
from jax.sharding import PartitionSpec as P


def on_device(
    features, sketch_matrix, tiles, tile_dst, tile_src, halo_index, send_order, arrival_place
):
    sketched = lax.dot_general(
        sketch_matrix, features, (((0,), (1,)), ((), ())), preferred_element_type=jnp.float32
    ).astype(jnp.bfloat16)
    hop0 = lax.all_to_all(sketched, "rep", split_axis=0, concat_axis=1, tiled=True)
    tile_set = tiles[0]
    targets = tile_dst[0]
    sources = tile_src[0]
    halo_rows = halo_index[0]
    order = send_order[0]
    place = arrival_place[0]
    channels, node_count = hop0.shape
    tile_size = tile_set.shape[-1]
    block_count = node_count // tile_size
    onehot = (targets[:, None] == jnp.arange(block_count, dtype=jnp.int32)[None, :]).astype(
        jnp.float32
    )
    row_sums = jnp.sum(tile_set, axis=2, dtype=jnp.float32)
    degree = jnp.einsum("ti,tb->bi", row_sums, onehot, precision=lax.Precision.HIGHEST).reshape(
        node_count
    )

    def combine(layer, received):
        columns = jnp.concatenate([layer, received], 1)
        blocks = columns.reshape(channels, -1, tile_size)[:, sources, :]
        products = jnp.einsum("ctj,tij->cti", blocks, tile_set, preferred_element_type=jnp.float32)
        summed = jnp.einsum("cti,tb->cbi", products, onehot, precision=lax.Precision.HIGHEST)
        summed = summed.reshape(channels, node_count)
        return (summed / degree[None, :]).astype(jnp.bfloat16)

    hop1 = combine(
        hop0, lax.all_to_all(hop0[:, halo_rows], "dom", split_axis=1, concat_axis=1, tiled=True)
    )
    hop2 = combine(
        hop1, lax.all_to_all(hop1[:, halo_rows], "dom", split_axis=1, concat_axis=1, tiled=True)
    )
    stacked = jnp.concatenate([hop0, hop1, hop2], 0)[:, order]
    arrived = lax.all_to_all(stacked, "dom", split_axis=1, concat_axis=1, tiled=True)
    placed = jnp.zeros_like(arrived).at[:, place].set(arrived)
    return placed.reshape(3, channels, node_count)


def solution(mesh):
    in_specs = (
        P(("dom", "rep"), None),
        P(),
        P("dom", None, None, None),
        P("dom", None),
        P("dom", None),
        P("dom", None),
        P("dom", None),
        P("dom", None),
    )
    out_specs = P(None, "rep", "dom")
    return jax.shard_map(
        on_device, mesh=mesh, in_specs=in_specs, out_specs=out_specs, check_vma=False
    )
```

profile of v0, /device:TPU:0, one launch (start us, length us, event | category | flops | bytes accessed | tf_op | source)
XLA Modules:
  0.0 109.8 jit_solution(15514057003822116897)
XLA Ops:
  0.0 0.0 copy-start
  0.0 0.0 copy-start.10
  0.0 1.1 %copy-done = bf16[512,768]{1,0:T(8,128)(2,1)S(1)} copy-done((bf16[512,768]{1,0:T(8,128)(2,1)S(1)}, bf16[512,768]{1,0:T(8,128)(2,1)}, u32[]{:S(2)}) %copy-start) | copy-done | bytes 786456
  1.1 2.1 %convolution_convert_fusion = bf16[256,512]{1,0:T(8,128)(2,1)} fusion(bf16[768,256]{1,0:T(8,128)(2,1)} %param.9, bf16[512,768]{1,0:T(8,128)(2,1)S(1)} %copy-done), kind=kOutput, calls=%fused_computation.17 | convolution fusion | flops 201457664 | bytes 1441792 | tf_op jit(solution)/shard_map/dot_general | solution.py:10
  3.3 0.0 copy-start.8
  3.3 4.4 %all-to-all-start = ((bf16[4,64,512]{2,1,0:T(8,128)(2,1)}), bf16[4,64,512]{2,1,0:T(8,128)(2,1)S(1)}, u32[]{:S(2)}, u32[]{:S(2)}) async-start(bf16[4,64,512]{2,1,0:T(8,128)(2,1)} %bitcast.2), calls=%async_computation | async-start | bytes 524288 | tf_op jit(solution)/shard_map/all_to_all | solution.py:13
  7.6 0.0 copy-done.10
  7.6 2.5 %convert_reduce_fusion = f32[20,256]{1,0:T(8,128)S(1)} fusion(bf16[1,20,256,256]{3,2,1,0:T(8,128)(2,1)} %param.10), kind=kLoop, calls=%fused_computation.6 | loop fusion | flops 2616320 | bytes 2641920 | tf_op jit(solution)/shard_map/reduce_sum | solution.py:26
  10.1 0.0 copy-done.8
  10.1 0.1 convolution_bitcast_fusion
  10.3 3.3 %all-to-all-done = bf16[4,64,512]{2,1,0:T(8,128)(2,1)S(1)} async-done(((bf16[4,64,512]{2,1,0:T(8,128)(2,1)}), bf16[4,64,512]{2,1,0:T(8,128)(2,1)S(1)}, u32[]{:S(2)}, u32[]{:S(2)}) %all-to-all-start) | async-done | bytes 262176 | tf_op jit(solution)/shard_map/all_to_all | solution.py:13
  13.6 0.0 copy-start.11
  13.7 0.0 copy-start.3
  13.7 0.3 copy.76
  13.9 3.2 %gather_fusion = bf16[1024,64]{1,0:T(8,128)(2,1)S(1)} fusion(bf16[64,2048]{0,1:T(8,128)(2,1)S(1)} %copy.76, s32[1024]{0:T(1024)S(1)} %broadcast_clamp_fusion.1), kind=kCustom, calls=%fused_computation | custom fusion | bytes 266240 | tf_op jit(solution)/shard_map/gather | solution.py:40
  17.2 0.8 copy.77
  17.9 6.5 %all-to-all-start.1 = ((bf16[64,8,128]{2,0,1:T(8,128)(2,1)}), bf16[64,8,128]{2,0,1:T(8,128)(2,1)S(1)}, u32[]{:S(2)}, u32[]{:S(2)}) async-start(bf16[64,8,128]{2,0,1:T(8,128)(2,1)} %copy.77), calls=%async_computation.1 | async-start | bytes 262144 | tf_op jit(solution)/shard_map/all_to_all | solution.py:40
  24.4 0.0 copy-done.11
  24.4 0.0 copy-start.7
  24.4 7.3 %all-to-all-done.1 = bf16[64,8,128]{2,0,1:T(8,128)(2,1)S(1)} async-done(((bf16[64,8,128]{2,0,1:T(8,128)(2,1)}), bf16[64,8,128]{2,0,1:T(8,128)(2,1)S(1)}, u32[]{:S(2)}, u32[]{:S(2)}) %all-to-all-start.1) | async-done | bytes 131104 | tf_op jit(solution)/shard_map/all_to_all | solution.py:40
  31.7 0.0 copy-done.3
  31.8 0.0 copy-start.1
  31.8 1.1 %pad_maximum_fusion.1 = bf16[64,3072]{1,0:T(8,128)(2,1)S(1)} fusion(bf16[64,1024]{1,0:T(8,128)(2,1)S(1)} %copy_bitcast_fusion.3, bf16[64,2048]{1,0:T(8,128)(2,1)} %bitcast.87), kind=kLoop, calls=%fused_computation.28 | loop fusion | flops 786432 | bytes 786432 | tf_op jit(solution)/shard_map/concatenate | solution.py:32
  32.9 0.8 copy.109
  33.7 2.5 %gather_fusion.1 = bf16[20,64,256]{2,1,0:T(8,128)(2,1)} fusion(bf16[64,12,256]{2,0,1:T(8,128)(2,1)} %bitcast.90, s32[1024]{0:T(1024)S(1)} %pad_clamp_fusion), kind=kCustom, calls=%fused_computation.1 | custom fusion | bytes 1310800 | tf_op jit(solution)/shard_map/gather | solution.py:33
  36.1 0.0 copy-done.7
  36.1 0.0 copy-done.1
  36.2 2.0 %fusion.8 = f32[64,20,256]{2,0,1:T(8,128)S(1)} fusion(bf16[1,20,256,256]{3,2,1,0:T(8,128)(2,1)S(1)} %copy-done.1, bf16[20,64,256]{2,1,0:T(8,128)(2,1)} %gather_fusion.1), kind=kOutput, calls=%fused_computation.15 | convolution fusion | flops 167772160 | bytes 4587520 | tf_op jit(solution)/shard_map/ctj,tij->cti/dot_general | solution.py:34
  38.1 1.3 %fusion.6 = f32[8,64,256]{2,0,1:T(8,128)S(1)} fusion(f32[64,20,256]{2,0,1:T(8,128)S(1)} %fusion.8, s32[20]{0:T(128)S(1)} %bitcast.109), kind=kOutput, calls=%fused_computation.13 | convolution fusion | flops 31457440 | bytes 1835088 | tf_op jit(solution)/shard_map/cti,tb->cbi/dot_general | solution.py:35
  39.5 0.2 copy.97
  39.6 0.0 copy-start.5
  39.7 0.7 divide_convert_fusion.1
  40.4 2.0 %copy.81 = bf16[64,2048]{0,1:T(8,128)(2,1)} copy(bf16[64,2048]{1,0:T(8,128)(2,1)} %divide_convert_fusion.1) | data formatting | bytes 524288 | tf_op jit(solution)/shard_map/convert_element_type | solution.py:37
  42.3 5.1 %gather_fusion.2 = bf16[1024,64]{1,0:T(8,128)(2,1)} fusion(bf16[64,2048]{0,1:T(8,128)(2,1)} %copy.81, s32[1024]{0:T(1024)S(1)} %broadcast_clamp_fusion.1), kind=kCustom, calls=%fused_computation.2 | custom fusion | bytes 266240 | tf_op jit(solution)/shard_map/gather | solution.py:43
  47.5 1.7 %copy.82 = bf16[64,8,128]{2,0,1:T(8,128)(2,1)} copy(bf16[64,8,128]{0,2,1:T(8,128)(2,1)} %bitcast.101) | data formatting | bytes 262144 | tf_op jit(solution)/shard_map/all_to_all | solution.py:43
  49.2 3.4 %all-to-all-start.2 = ((bf16[64,8,128]{2,0,1:T(8,128)(2,1)}), bf16[64,8,128]{2,0,1:T(8,128)(2,1)S(1)}, u32[]{:S(2)}, u32[]{:S(2)}) async-start(bf16[64,8,128]{2,0,1:T(8,128)(2,1)} %copy.82), calls=%async_computation.2 | async-start | bytes 262144 | tf_op jit(solution)/shard_map/all_to_all | solution.py:43
  52.6 0.0 copy-done.5
  52.6 7.2 %all-to-all-done.2 = bf16[64,8,128]{2,0,1:T(8,128)(2,1)S(1)} async-done(((bf16[64,8,128]{2,0,1:T(8,128)(2,1)}), bf16[64,8,128]{2,0,1:T(8,128)(2,1)S(1)}, u32[]{:S(2)}, u32[]{:S(2)}) %all-to-all-start.2) | async-done | bytes 131104 | tf_op jit(solution)/shard_map/all_to_all | solution.py:43
  59.9 1.0 pad_maximum_fusion.2
  60.9 0.8 copy.108
  61.7 2.6 %gather_fusion.3 = bf16[20,64,256]{2,1,0:T(8,128)(2,1)} fusion(bf16[64,12,256]{2,0,1:T(8,128)(2,1)} %bitcast.89, s32[1024]{0:T(1024)} %copy-done.7), kind=kCustom, calls=%fused_computation.3 | custom fusion | bytes 1310800 | tf_op jit(solution)/shard_map/gather | solution.py:33
  64.2 0.0 copy-start.9
  64.2 2.0 %fusion.11 = f32[64,20,256]{2,0,1:T(8,128)S(1)} fusion(bf16[1,20,256,256]{3,2,1,0:T(8,128)(2,1)S(1)} %copy-done.1, bf16[20,64,256]{2,1,0:T(8,128)(2,1)} %gather_fusion.3), kind=kOutput, calls=%fused_computation.16 | convolution fusion | flops 167772160 | bytes 4587520 | tf_op jit(solution)/shard_map/ctj,tij->cti/dot_general | solution.py:34
  66.2 0.0 copy-done.9
  66.2 0.0 copy-start.2
  66.3 0.0 copy-start.4
  66.3 1.3 %fusion.4 = f32[8,64,256]{2,0,1:T(8,128)S(1)} fusion(f32[64,20,256]{2,0,1:T(8,128)S(1)} %fusion.11, s32[20]{0:T(128)S(1)} %bitcast.110), kind=kOutput, calls=%fused_computation.11 | convolution fusion | flops 31457440 | bytes 1835088 | tf_op jit(solution)/shard_map/cti,tb->cbi/dot_general | solution.py:35
  67.6 0.2 copy.99
  67.8 0.0 copy-done.2
  67.8 0.0 copy-done.4
  67.8 0.1 pad_maximum_fusion
  67.9 0.5 copy.86
  68.4 7.5 %gather_fusion.4 = bf16[2048,192]{1,0:T(8,128)(2,1)S(1)} fusion(bf16[192,2048]{0,1:T(8,128)(2,1)S(1)} %copy.86, s32[2048]{0:T(1024)S(1)} %broadcast_clamp_fusion), kind=kCustom, calls=%fused_computation.4 | custom fusion | bytes 1581056 | tf_op jit(solution)/shard_map/gather | solution.py:45
  75.9 0.0 copy-start.6
  75.9 1.3 %copy.87 = bf16[192,8,256]{2,0,1:T(8,128)(2,1)} copy(bf16[192,8,256]{0,2,1:T(8,128)(2,1)S(1)} %bitcast.91) | data formatting | bytes 1572864 | tf_op jit(solution)/shard_map/all_to_all | solution.py:46
  77.2 3.5 %all-to-all-start.3 = ((bf16[192,8,256]{2,0,1:T(8,128)(2,1)}), bf16[192,8,256]{2,0,1:T(8,128)(2,1)S(1)}, u32[]{:S(2)}, u32[]{:S(2)}) async-start(bf16[192,8,256]{2,0,1:T(8,128)(2,1)} %copy.87), calls=%async_computation.3 | async-start | bytes 1572864 | tf_op jit(solution)/shard_map/all_to_all | solution.py:46
  80.8 0.0 copy-done.6
  80.8 17.5 %all-to-all-done.3 = bf16[192,8,256]{2,0,1:T(8,128)(2,1)S(1)} async-done(((bf16[192,8,256]{2,0,1:T(8,128)(2,1)}), bf16[192,8,256]{2,0,1:T(8,128)(2,1)S(1)}, u32[]{:S(2)}, u32[]{:S(2)}) %all-to-all-start.3) | async-done | bytes 786464 | tf_op jit(solution)/shard_map/all_to_all | solution.py:46
  98.3 0.1 copy.96
  98.4 0.5 copy.89
  98.9 9.6 %scatter_custom_fusion = bf16[192,2048]{0,1:T(8,128)(2,1)S(1)} fusion(s32[2048]{0:T(1024)S(1)} %bitcast.107, bf16[2048,192]{1,0:T(8,128)(2,1)S(1)} %copy.89, bf16[]{:T(256)} %constant.5.clone.1), kind=kCustom, calls=%fused_computation.24 | custom fusion | bytes 786434 | tf_op jit(solution)/shard_map/scatter | solution.py:47
  108.5 1.2 %copy.90 = bf16[192,2048]{1,0:T(8,128)(2,1)} copy(bf16[192,2048]{0,1:T(8,128)(2,1)S(1)} %scatter_custom_fusion) | data formatting | bytes 1572864 | tf_op jit(solution)/shard_map/scatter | solution.py:47
  (12 shorter events, 0.2 us)
Async XLA Ops:
  0.0 1.1 %copy-start = (bf16[512,768]{1,0:T(8,128)(2,1)S(1)}, bf16[512,768]{1,0:T(8,128)(2,1)}, u32[]{:S(2)}) copy-start(bf16[512,768]{1,0:T(8,128)(2,1)} %param.8) | copy-start | bytes 2359300
  0.0 7.6 %copy-start.10 = (s32[1,1024]{1,0:T(1,128)S(1)}, s32[1,1024]{1,0:T(1,128)}, u32[]{:S(2)}) copy-start(s32[1,1024]{1,0:T(1,128)} %param.13) | copy-start | bytes 12292
  3.3 6.9 %copy-start.8 = (s32[1,20]{1,0:T(1,128)S(1)}, s32[1,20]{1,0:T(1,128)}, u32[]{:S(2)}) copy-start(s32[1,20]{1,0:T(1,128)} %param.11) | copy-start | bytes 244
  3.3 10.4 %all-to-all-start = ((bf16[4,64,512]{2,1,0:T(8,128)(2,1)}), bf16[4,64,512]{2,1,0:T(8,128)(2,1)S(1)}, u32[]{:S(2)}, u32[]{:S(2)}) async-start(bf16[4,64,512]{2,1,0:T(8,128)(2,1)} %bitcast.2), calls=%async_computation | async-start | bytes 524288 | tf_op jit(solution)/shard_map/all_to_all | solution.py:13
  13.6 10.8 %copy-start.11 = (s32[1,20]{1,0:T(1,128)S(1)}, s32[1,20]{1,0:T(1,128)}, u32[]{:S(2)}) copy-start(s32[1,20]{1,0:T(1,128)} %param.12) | copy-start | bytes 244
  13.7 18.1 %copy-start.3 = (bf16[4,8,8,512]{3,2,0,1:T(8,128)(2,1)}, bf16[4,8,8,512]{3,2,0,1:T(8,128)(2,1)S(1)}, u32[]{:S(2)}) copy-start(bf16[4,8,8,512]{3,2,0,1:T(8,128)(2,1)S(1)} %copy.93) | copy-start | bytes 786436
  17.9 13.8 %all-to-all-start.1 = ((bf16[64,8,128]{2,0,1:T(8,128)(2,1)}), bf16[64,8,128]{2,0,1:T(8,128)(2,1)S(1)}, u32[]{:S(2)}, u32[]{:S(2)}) async-start(bf16[64,8,128]{2,0,1:T(8,128)(2,1)} %copy.77), calls=%async_computation.1 | async-start | bytes 262144 | tf_op jit(solution)/shard_map/all_to_all | solution.py:40
  24.4 11.7 %copy-start.7 = (s32[1024]{0:T(1024)}, s32[1024]{0:T(1024)S(1)}, u32[]{:S(2)}) copy-start(s32[1024]{0:T(1024)S(1)} %pad_clamp_fusion) | copy-start | bytes 12292
  31.8 4.4 %copy-start.1 = (bf16[1,20,256,256]{3,2,1,0:T(8,128)(2,1)S(1)}, bf16[1,20,256,256]{3,2,1,0:T(8,128)(2,1)}, u32[]{:S(2)}) copy-start(bf16[1,20,256,256]{3,2,1,0:T(8,128)(2,1)} %param.10) | copy-start | bytes 7864324
  39.6 13.0 %copy-start.5 = (s32[1,2048]{1,0:T(1,128)S(1)}, s32[1,2048]{1,0:T(1,128)}, u32[]{:S(2)}) copy-start(s32[1,2048]{1,0:T(1,128)} %param.14) | copy-start | bytes 24580
  49.2 10.7 %all-to-all-start.2 = ((bf16[64,8,128]{2,0,1:T(8,128)(2,1)}), bf16[64,8,128]{2,0,1:T(8,128)(2,1)S(1)}, u32[]{:S(2)}, u32[]{:S(2)}) async-start(bf16[64,8,128]{2,0,1:T(8,128)(2,1)} %copy.82), calls=%async_computation.2 | async-start | bytes 262144 | tf_op jit(solution)/shard_map/all_to_all | solution.py:43
  64.2 2.0 %copy-start.9 = (s32[1,20]{1,0:T(1,128)S(1)}, s32[1,20]{1,0:T(1,128)}, u32[]{:S(2)}) copy-start(s32[1,20]{1,0:T(1,128)} %param.11) | copy-start | bytes 244
  66.2 1.6 %copy-start.2 = (bf16[64,2048]{1,0:T(8,128)(2,1)S(1)}, bf16[64,2048]{1,0:T(8,128)(2,1)}, u32[]{:S(2)}) copy-start(bf16[64,2048]{1,0:T(8,128)(2,1)} %divide_convert_fusion.1) | copy-start | bytes 786436
  66.3 1.6 %copy-start.4 = (bf16[4,8,8,512]{3,2,0,1:T(8,128)(2,1)S(1)}, bf16[4,8,8,512]{3,2,0,1:T(8,128)(2,1)}, u32[]{:S(2)}) copy-start(bf16[4,8,8,512]{3,2,0,1:T(8,128)(2,1)} %copy-done.3) | copy-start | bytes 786436
  75.9 4.8 %copy-start.6 = (s32[1,2048]{1,0:T(1,128)S(1)}, s32[1,2048]{1,0:T(1,128)}, u32[]{:S(2)}) copy-start(s32[1,2048]{1,0:T(1,128)} %param.15) | copy-start | bytes 24580
  77.2 21.1 %all-to-all-start.3 = ((bf16[192,8,256]{2,0,1:T(8,128)(2,1)}), bf16[192,8,256]{2,0,1:T(8,128)(2,1)S(1)}, u32[]{:S(2)}, u32[]{:S(2)}) async-start(bf16[192,8,256]{2,0,1:T(8,128)(2,1)} %copy.87), calls=%async_computation.3 | async-start | bytes 1572864 | tf_op jit(solution)/shard_map/all_to_all | solution.py:46
where the time goes:
time: 111 us; the launch traced here: 110 us
  local copies, waits for them, and re-layouts  41.9 us (38%)
  waiting for transfers between devices  35.4 us (32%)
  starting transfers between devices  17.7 us (16%)
  matrix products  8.87 us (8%)
  other arithmetic  5.49 us (5%)
    all_to_all x1, waiting for transfers between devices, on_device(): lax.all_to_all(stacked, 'dom', split_axis=1, concat_axis=1, tiled=True)  17.5 us
    scatter x2, local copies, waits for them, and re-layouts, on_device(): placed = jnp.zeros_like(arrived).at[:, place].set(arrived)  10.8 us
    gather x1, local copies, waits for them, and re-layouts, on_device(): stacked = jnp.concatenate([hop0, hop1, hop2], 0)[:, order]  7.5 us
    all_to_all x1, waiting for transfers between devices, on_device(): lax.all_to_all(hop0[:, halo_rows], 'dom', split_axis=1, concat_axis=1, ti...  7.3 us
    all_to_all x1, waiting for transfers between devices, on_device(): lax.all_to_all(hop1[:, halo_rows], 'dom', split_axis=1, concat_axis=1, ti...  7.24 us
    all_to_all x1, starting transfers between devices, on_device(): lax.all_to_all(hop0[:, halo_rows], 'dom', split_axis=1, concat_axis=1, ti...  6.46 us
    gather x1, local copies, waits for them, and re-layouts, on_device(): hop1[:, halo_rows]  5.14 us
    gather x2, local copies, waits for them, and re-layouts, combine(): blocks = columns.reshape(channels, -1, tile_size)[:, sources, :]  5.03 us
  transfers between devices with their start and end apart: 4, of which 4 were waited for; matrix products, arithmetic and copies ran while one was open for 2% of the time, Pallas kernels for 0%

commit v1 on v0

--- a/solution.py
+++ b/solution.py
@@ -43,7 +43,10 @@
         hop1, lax.all_to_all(hop1[:, halo_rows], "dom", split_axis=1, concat_axis=1, tiled=True)
     )
     stacked = jnp.concatenate([hop0, hop1, hop2], 0)[:, order]
-    arrived = lax.all_to_all(stacked, "dom", split_axis=1, concat_axis=1, tiled=True)
+    arrived = jnp.concatenate(
+        lax.all_to_all(jnp.stack(jnp.split(stacked, lax.axis_size("dom"), axis=1)), "dom", 0, 0),
+        axis=1,
+    )
     placed = jnp.zeros_like(arrived).at[:, place].set(arrived)
     return placed.reshape(3, channels, node_count)
 

time: 111 us -> 118 us (1.063)
  local copies, waits for them, and re-layouts: 41.9 us -> 49.2 us
  other arithmetic: 5.49 us -> 4.3 us
    all_to_all x2, local copies, waits for them, and re-layouts: 0.29 us -> 3.78 us  [on_device(): lax.all_to_all(sketched, 'rep', split_axis=0, concat_axis=1, tiled=True)]
    all_to_all x1, waiting for transfers between devices: 3.34 us -> 5.95 us  [on_device(): lax.all_to_all(sketched, 'rep', split_axis=0, concat_axis=1, tiled=True)]
    gather x1, local copies, waits for them, and re-layouts: 3.21 us -> 5.17 us  [on_device(): hop0[:, halo_rows]]
    all_to_all x3 -> x0, local copies, waits for them, and re-layouts: 1.85 us -> none  [on_device(): lax.all_to_all(stacked, 'dom', split_axis=1, concat_axis=1, tiled=True)]
    reduce_sum x1, other arithmetic: 2.49 us -> 0.75 us  [on_device(): row_sums = jnp.sum(tile_set, axis=2, dtype=jnp.float32)]
    another operation x0 -> x2, local copies, waits for them, and re-layouts: none -> 1.27 us  [on_device(): jnp.stack(jnp.split(stacked, lax.axis_size('dom'), axis=1))]
  transfers between devices with their start and end apart: 4 -> 4, of which waited for: 4 -> 4; matrix products, arithmetic and copies ran while one was open for 2% -> 1% of each run, Pallas kernels for 0% -> 0%
where the time goes in v1:
time: 118 us; the launch traced here: 117 us
  local copies, waits for them, and re-layouts  49.2 us (42%)
  waiting for transfers between devices  36.5 us (31%)
  starting transfers between devices  17.6 us (15%)
  matrix products  8.87 us (8%)
  other arithmetic  4.3 us (4%)
    all_to_all x1, waiting for transfers between devices, on_device(): lax.all_to_all(jnp.stack(jnp.split(stacked, lax.axis_size('dom'), axis=1)...  17.5 us
    scatter x2, local copies, waits for them, and re-layouts, on_device(): placed = jnp.zeros_like(arrived).at[:, place].set(arrived)  10.8 us
    gather x1, local copies, waits for them, and re-layouts, on_device(): stacked = jnp.concatenate([hop0, hop1, hop2], 0)[:, order]  7.5 us
    all_to_all x1, waiting for transfers between devices, on_device(): lax.all_to_all(hop1[:, halo_rows], 'dom', split_axis=1, concat_axis=1, ti...  6.56 us
    all_to_all x1, starting transfers between devices, on_device(): lax.all_to_all(hop0[:, halo_rows], 'dom', split_axis=1, concat_axis=1, ti...  6.45 us
    all_to_all x1, waiting for transfers between devices, on_device(): lax.all_to_all(hop0[:, halo_rows], 'dom', split_axis=1, concat_axis=1, ti...  6.44 us
    all_to_all x1, waiting for transfers between devices, on_device(): lax.all_to_all(sketched, 'rep', split_axis=0, concat_axis=1, tiled=True)  5.95 us
    gather x1, local copies, waits for them, and re-layouts, on_device(): hop0[:, halo_rows]  5.17 us
  transfers between devices with their start and end apart: 4, of which 4 were waited for; matrix products, arithmetic and copies ran while one was open for 1% of the time, Pallas kernels for 0%

profile of v1, /device:TPU:0, one launch (start us, length us, event | category | flops | bytes accessed | tf_op | source)
XLA Modules:
  0.0 116.8 jit_solution(15374844775916884746)
XLA Ops:
  0.0 0.0 copy-start
  0.0 0.0 copy-start.10
  0.0 0.0 copy-start.11
  0.0 1.1 copy-done
  1.1 2.1 %convolution_convert_fusion = bf16[256,512]{1,0:T(8,128)(2,1)} fusion(bf16[768,256]{1,0:T(8,128)(2,1)} %param.9, bf16[512,768]{1,0:T(8,128)(2,1)S(1)} %copy-done), kind=kOutput, calls=%fused_computation.17 | convolution fusion | flops 201457664 | bytes 1441792 | tf_op jit(solution)/shard_map/dot_general | solution.py:10
  3.3 4.2 %all-to-all-start = ((bf16[4,64,512]{2,1,0:T(8,128)(2,1)}), bf16[4,64,512]{2,1,0:T(8,128)(2,1)S(1)}, u32[]{:S(2)}, u32[]{:S(2)}) async-start(bf16[4,64,512]{2,1,0:T(8,128)(2,1)} %bitcast.2), calls=%async_computation | async-start | bytes 524288 | tf_op jit(solution)/shard_map/all_to_all | solution.py:13
  7.5 0.0 copy-done.10
  7.5 0.0 copy-done.11
  7.5 0.0 copy-start.6
  7.5 5.9 %all-to-all-done = bf16[4,64,512]{2,1,0:T(8,128)(2,1)S(1)} async-done(((bf16[4,64,512]{2,1,0:T(8,128)(2,1)}), bf16[4,64,512]{2,1,0:T(8,128)(2,1)S(1)}, u32[]{:S(2)}, u32[]{:S(2)}) %all-to-all-start) | async-done | bytes 262176 | tf_op jit(solution)/shard_map/all_to_all | solution.py:13
  13.5 0.0 copy-start.4
  13.5 0.7 copy-done.4
  14.2 0.0 copy-start.1
  14.2 1.8 %copy.93 = bf16[4,8,8,512]{3,2,0,1:T(8,128)(2,1)} copy(bf16[4,8,8,512]{3,2,1,0:T(8,128)(2,1)} %bitcast.138) | data formatting | bytes 524288 | tf_op jit(solution)/shard_map/all_to_all | solution.py:13
  16.0 2.0 %copy.76 = bf16[64,2048]{0,1:T(8,128)(2,1)} copy(bf16[64,2048]{1,0:T(8,128)(2,1)} %bitcast.117) | data formatting | bytes 524288 | tf_op jit(solution)/shard_map/all_to_all | solution.py:13
  18.0 5.2 %gather_fusion = bf16[1024,64]{1,0:T(8,128)(2,1)} fusion(bf16[64,2048]{0,1:T(8,128)(2,1)} %copy.76, s32[1024]{0:T(1024)S(1)} %get-tuple-element.6), kind=kCustom, calls=%fused_computation | custom fusion | bytes 266240 | tf_op jit(solution)/shard_map/gather | solution.py:40
  23.2 0.0 copy-start.7
  23.2 1.7 %copy.77 = bf16[64,8,128]{2,0,1:T(8,128)(2,1)} copy(bf16[64,8,128]{0,2,1:T(8,128)(2,1)} %bitcast.140) | data formatting | bytes 262144 | tf_op jit(solution)/shard_map/all_to_all | solution.py:40
  24.9 6.5 %all-to-all-start.1 = ((bf16[64,8,128]{2,0,1:T(8,128)(2,1)}), bf16[64,8,128]{2,0,1:T(8,128)(2,1)S(1)}, u32[]{:S(2)}, u32[]{:S(2)}) async-start(bf16[64,8,128]{2,0,1:T(8,128)(2,1)} %copy.77), calls=%async_computation.1 | async-start | bytes 262144 | tf_op jit(solution)/shard_map/all_to_all | solution.py:40
  31.4 0.0 copy-done.1
  31.4 0.7 convert_reduce_fusion
  32.1 0.0 copy-done.7
  32.1 0.1 convolution_bitcast_fusion
  32.3 6.4 %all-to-all-done.1 = bf16[64,8,128]{2,0,1:T(8,128)(2,1)S(1)} async-done(((bf16[64,8,128]{2,0,1:T(8,128)(2,1)}), bf16[64,8,128]{2,0,1:T(8,128)(2,1)S(1)}, u32[]{:S(2)}, u32[]{:S(2)}) %all-to-all-start.1) | async-done | bytes 131104 | tf_op jit(solution)/shard_map/all_to_all | solution.py:40
  38.7 1.0 pad_maximum_fusion.1
  39.7 0.8 copy.109
  40.5 2.5 %gather_fusion.1 = bf16[20,64,256]{2,1,0:T(8,128)(2,1)} fusion(bf16[64,12,256]{2,0,1:T(8,128)(2,1)} %bitcast.120, s32[1024]{0:T(1024)S(1)} %get-tuple-element.5), kind=kCustom, calls=%fused_computation.1 | custom fusion | bytes 1310800 | tf_op jit(solution)/shard_map/gather | solution.py:33
  42.9 0.0 copy-start.8
  42.9 2.0 %fusion.8 = f32[64,20,256]{2,0,1:T(8,128)S(1)} fusion(bf16[1,20,256,256]{3,2,1,0:T(8,128)(2,1)S(1)} %copy-done.1, bf16[20,64,256]{2,1,0:T(8,128)(2,1)} %gather_fusion.1), kind=kOutput, calls=%fused_computation.15 | convolution fusion | flops 167772160 | bytes 4587520 | tf_op jit(solution)/shard_map/ctj,tij->cti/dot_general | solution.py:34
  44.9 0.0 copy-done.6
  45.0 0.0 copy-done.8
  45.0 1.3 %fusion.6 = f32[8,64,256]{2,0,1:T(8,128)S(1)} fusion(f32[64,20,256]{2,0,1:T(8,128)S(1)} %fusion.8, s32[20]{0:T(128)S(1)} %bitcast.147), kind=kOutput, calls=%fused_computation.13 | convolution fusion | flops 31457440 | bytes 1835088 | tf_op jit(solution)/shard_map/cti,tb->cbi/dot_general | solution.py:35
  46.3 0.2 copy.97
  46.5 0.7 divide_convert_fusion.1
  47.2 2.0 %copy.81 = bf16[64,2048]{0,1:T(8,128)(2,1)} copy(bf16[64,2048]{1,0:T(8,128)(2,1)} %divide_convert_fusion.1) | data formatting | bytes 524288 | tf_op jit(solution)/shard_map/convert_element_type | solution.py:37
  49.2 5.2 %gather_fusion.2 = bf16[1024,64]{1,0:T(8,128)(2,1)} fusion(bf16[64,2048]{0,1:T(8,128)(2,1)} %copy.81, s32[1024]{0:T(1024)S(1)} %get-tuple-element.6), kind=kCustom, calls=%fused_computation.2 | custom fusion | bytes 266240 | tf_op jit(solution)/shard_map/gather | solution.py:43
  54.3 1.7 %copy.82 = bf16[64,8,128]{2,0,1:T(8,128)(2,1)} copy(bf16[64,8,128]{0,2,1:T(8,128)(2,1)} %bitcast.139) | data formatting | bytes 262144 | tf_op jit(solution)/shard_map/all_to_all | solution.py:43
  56.1 3.4 %all-to-all-start.2 = ((bf16[64,8,128]{2,0,1:T(8,128)(2,1)}), bf16[64,8,128]{2,0,1:T(8,128)(2,1)S(1)}, u32[]{:S(2)}, u32[]{:S(2)}) async-start(bf16[64,8,128]{2,0,1:T(8,128)(2,1)} %copy.82), calls=%async_computation.2 | async-start | bytes 262144 | tf_op jit(solution)/shard_map/all_to_all | solution.py:43
  59.4 0.7 compare_select_fusion
  60.2 6.6 %all-to-all-done.2 = bf16[64,8,128]{2,0,1:T(8,128)(2,1)S(1)} async-done(((bf16[64,8,128]{2,0,1:T(8,128)(2,1)}), bf16[64,8,128]{2,0,1:T(8,128)(2,1)S(1)}, u32[]{:S(2)}, u32[]{:S(2)}) %all-to-all-start.2) | async-done | bytes 131104 | tf_op jit(solution)/shard_map/all_to_all | solution.py:43
  66.7 1.0 pad_maximum_fusion.2
  67.7 0.8 copy.108
  68.5 2.6 %gather_fusion.3 = bf16[20,64,256]{2,1,0:T(8,128)(2,1)} fusion(bf16[64,12,256]{2,0,1:T(8,128)(2,1)} %bitcast.121, s32[1024]{0:T(1024)} %copy-done.6), kind=kCustom, calls=%fused_computation.3 | custom fusion | bytes 1310800 | tf_op jit(solution)/shard_map/gather | solution.py:33
  71.1 0.0 copy-start.9
  71.1 2.0 %fusion.11 = f32[64,20,256]{2,0,1:T(8,128)S(1)} fusion(bf16[1,20,256,256]{3,2,1,0:T(8,128)(2,1)S(1)} %copy-done.1, bf16[20,64,256]{2,1,0:T(8,128)(2,1)} %gather_fusion.3), kind=kOutput, calls=%fused_computation.16 | convolution fusion | flops 167772160 | bytes 4587520 | tf_op jit(solution)/shard_map/ctj,tij->cti/dot_general | solution.py:34
  73.1 0.0 copy-done.9
  73.1 0.0 copy-start.2
  73.1 0.0 copy-start.3
  73.1 1.3 %fusion.4 = f32[8,64,256]{2,0,1:T(8,128)S(1)} fusion(f32[64,20,256]{2,0,1:T(8,128)S(1)} %fusion.11, s32[20]{0:T(128)S(1)} %bitcast.148), kind=kOutput, calls=%fused_computation.11 | convolution fusion | flops 31457440 | bytes 1835088 | tf_op jit(solution)/shard_map/cti,tb->cbi/dot_general | solution.py:35
  74.4 0.2 copy.99
  74.7 0.0 copy-done.2
  74.7 0.0 copy-done.3
  74.7 0.1 pad_maximum_fusion
  74.8 0.5 copy.86
  75.3 7.5 %gather_fusion.4 = bf16[2048,192]{1,0:T(8,128)(2,1)S(1)} fusion(bf16[192,2048]{0,1:T(8,128)(2,1)S(1)} %copy.86, s32[2048]{0:T(1024)S(1)} %broadcast_clamp_fusion), kind=kCustom, calls=%fused_computation.4 | custom fusion | bytes 1581056 | tf_op jit(solution)/shard_map/gather | solution.py:45
  82.9 0.0 copy-start.5
  83.0 1.3 %copy.87 = bf16[8,192,256]{2,1,0:T(8,128)(2,1)} copy(bf16[8,192,256]{1,2,0:T(8,128)(2,1)S(1)} %fusion.18) | data formatting | bytes 1572864 | tf_op jit(solution)/shard_map/stack | solution.py:47
  84.2 3.5 %all-to-all-start.3 = ((bf16[8,192,256]{2,1,0:T(8,128)(2,1)}), bf16[8,192,256]{2,1,0:T(8,128)(2,1)S(1)}, u32[]{:S(2)}, u32[]{:S(2)}) async-start(bf16[8,192,256]{2,1,0:T(8,128)(2,1)} %copy.87), calls=%async_computation.3 | async-start | bytes 1572864 | tf_op jit(solution)/shard_map/all_to_all | solution.py:47
  87.8 0.0 copy-done.5
  87.8 17.5 %all-to-all-done.3 = bf16[8,192,256]{2,1,0:T(8,128)(2,1)S(1)} async-done(((bf16[8,192,256]{2,1,0:T(8,128)(2,1)}), bf16[8,192,256]{2,1,0:T(8,128)(2,1)S(1)}, u32[]{:S(2)}, u32[]{:S(2)}) %all-to-all-start.3) | async-done | bytes 786464 | tf_op jit(solution)/shard_map/all_to_all | solution.py:47
  105.3 0.1 copy.96
  105.4 0.5 copy.89
  106.0 9.6 %scatter_custom_fusion = bf16[192,2048]{0,1:T(8,128)(2,1)S(1)} fusion(s32[2048]{0:T(1024)S(1)} %bitcast.145, bf16[2048,192]{1,0:T(8,128)(2,1)S(1)} %copy.89, bf16[]{:T(256)} %constant.5.clone.1), kind=kCustom, calls=%fused_computation.24 | custom fusion | bytes 786434 | tf_op jit(solution)/shard_map/scatter | solution.py:50
  115.5 1.2 %copy.90 = bf16[192,2048]{1,0:T(8,128)(2,1)} copy(bf16[192,2048]{0,1:T(8,128)(2,1)S(1)} %scatter_custom_fusion) | data formatting | bytes 1572864 | tf_op jit(solution)/shard_map/scatter | solution.py:50
  (17 shorter events, 0.2 us)
Async XLA Ops:
  0.0 1.1 copy-start
  0.0 7.5 %copy-start.10 = (s32[1,1024]{1,0:T(1,128)S(1)}, s32[1,1024]{1,0:T(1,128)}, u32[]{:S(2)}) copy-start(s32[1,1024]{1,0:T(1,128)} %param.13) | copy-start | bytes 12292
  0.0 7.5 %copy-start.11 = (s32[1,20]{1,0:T(1,128)S(1)}, s32[1,20]{1,0:T(1,128)}, u32[]{:S(2)}) copy-start(s32[1,20]{1,0:T(1,128)} %param.12) | copy-start | bytes 244
  3.3 10.2 %all-to-all-start = ((bf16[4,64,512]{2,1,0:T(8,128)(2,1)}), bf16[4,64,512]{2,1,0:T(8,128)(2,1)S(1)}, u32[]{:S(2)}, u32[]{:S(2)}) async-start(bf16[4,64,512]{2,1,0:T(8,128)(2,1)} %bitcast.2), calls=%async_computation | async-start | bytes 524288 | tf_op jit(solution)/shard_map/all_to_all | solution.py:13
  7.5 37.4 %copy-start.6 = (s32[1024]{0:T(1024)}, s32[1024]{0:T(1024)S(1)}, u32[]{:S(2)}) copy-start(s32[1024]{0:T(1024)S(1)} %get-tuple-element.5) | copy-start | bytes 12292
  13.5 0.7 copy-start.4
  14.2 17.2 %copy-start.1 = (bf16[1,20,256,256]{3,2,1,0:T(8,128)(2,1)S(1)}, bf16[1,20,256,256]{3,2,1,0:T(8,128)(2,1)}, u32[]{:S(2)}) copy-start(bf16[1,20,256,256]{3,2,1,0:T(8,128)(2,1)} %param.10) | copy-start | bytes 7864324
  23.2 9.0 %copy-start.7 = (s32[1,20]{1,0:T(1,128)S(1)}, s32[1,20]{1,0:T(1,128)}, u32[]{:S(2)}) copy-start(s32[1,20]{1,0:T(1,128)} %param.11) | copy-start | bytes 244
  24.9 13.8 %all-to-all-start.1 = ((bf16[64,8,128]{2,0,1:T(8,128)(2,1)}), bf16[64,8,128]{2,0,1:T(8,128)(2,1)S(1)}, u32[]{:S(2)}, u32[]{:S(2)}) async-start(bf16[64,8,128]{2,0,1:T(8,128)(2,1)} %copy.77), calls=%async_computation.1 | async-start | bytes 262144 | tf_op jit(solution)/shard_map/all_to_all | solution.py:40
  42.9 2.0 %copy-start.8 = (s32[1,20]{1,0:T(1,128)S(1)}, s32[1,20]{1,0:T(1,128)}, u32[]{:S(2)}) copy-start(s32[1,20]{1,0:T(1,128)} %param.11) | copy-start | bytes 244
  56.1 10.7 %all-to-all-start.2 = ((bf16[64,8,128]{2,0,1:T(8,128)(2,1)}), bf16[64,8,128]{2,0,1:T(8,128)(2,1)S(1)}, u32[]{:S(2)}, u32[]{:S(2)}) async-start(bf16[64,8,128]{2,0,1:T(8,128)(2,1)} %copy.82), calls=%async_computation.2 | async-start | bytes 262144 | tf_op jit(solution)/shard_map/all_to_all | solution.py:43
  71.1 2.0 %copy-start.9 = (s32[1,20]{1,0:T(1,128)S(1)}, s32[1,20]{1,0:T(1,128)}, u32[]{:S(2)}) copy-start(s32[1,20]{1,0:T(1,128)} %param.11) | copy-start | bytes 244
  73.1 1.6 %copy-start.2 = (bf16[64,2048]{1,0:T(8,128)(2,1)S(1)}, bf16[64,2048]{1,0:T(8,128)(2,1)}, u32[]{:S(2)}) copy-start(bf16[64,2048]{1,0:T(8,128)(2,1)} %divide_convert_fusion.1) | copy-start | bytes 786436
  73.1 1.6 %copy-start.3 = (bf16[4,8,8,512]{3,2,0,1:T(8,128)(2,1)S(1)}, bf16[4,8,8,512]{3,2,0,1:T(8,128)(2,1)}, u32[]{:S(2)}) copy-start(bf16[4,8,8,512]{3,2,0,1:T(8,128)(2,1)} %copy.93) | copy-start | bytes 786436
  82.9 4.8 %copy-start.5 = (s32[1,2048]{1,0:T(1,128)S(1)}, s32[1,2048]{1,0:T(1,128)}, u32[]{:S(2)}) copy-start(s32[1,2048]{1,0:T(1,128)} %param.15) | copy-start | bytes 24580
  84.2 21.1 %all-to-all-start.3 = ((bf16[8,192,256]{2,1,0:T(8,128)(2,1)}), bf16[8,192,256]{2,1,0:T(8,128)(2,1)S(1)}, u32[]{:S(2)}, u32[]{:S(2)}) async-start(bf16[8,192,256]{2,1,0:T(8,128)(2,1)} %copy.87), calls=%async_computation.3 | async-start | bytes 1572864 | tf_op jit(solution)/shard_map/all_to_all | solution.py:47
